TPU v7x, 32 devices: a whole 2x2x4 slice. The times are simulated.
32 devices in a mesh: dp: 2 (over y), expert: 16 (over z, x, core).
Axes of the slice: x: 2, y: 2, z: 4, core: 2. Of those that a mesh axis runs over, the one named last changes fastest.
Arguments:
- tokens: bfloat16 [2048, 3584], P('expert', 'dp'), may hold values from -6 to 6
- expert_ids: int32 [2048, 8], P('expert'), may hold values from 0 to 63, all different within a row; in each aligned block of 128 rows (0 to 127, 128 to 255, ...) at most 32 rows name the same one
- gate_weight: float32 [2048, 8], P('expert'), may hold values from 0.1 to 0.6
- w_gate: bfloat16 [16, 3584, 1024], P('expert', 'dp'), may hold values from -0.09375 to 0.09375
- w_up: bfloat16 [16, 3584, 1024], P('expert', 'dp'), may hold values from -0.09375 to 0.09375
- w_down: bfloat16 [16, 1024, 3584], P('expert', None, 'dp'), may hold values from -0.1875 to 0.1875
- grad_out: bfloat16 [2048, 3584], P('expert', 'dp'), may hold values from -6 to 6
Outputs:
- output: bfloat16 [2048, 3584], P('expert', 'dp')
- grad_tokens: bfloat16 [2048, 3584], P('expert', 'dp')
- grad_down: bfloat16 [16, 1024, 3584], P('expert', None, 'dp')
Inputs may be any that keep to these rules, and one draw needn't show every extreme that they name: `expert_ids`: each row names 8 different experts. Among the rows of one device no expert is named by more than 32 rows, and in some device's rows some expert is named by exactly 32 rows.
All inputs are finite; a program needn't handle non-finite values.
Results may differ from a plain program's by a relative error of at most 0.024.
Values may be sent and summed in bfloat16 or wider, within the bound.
A program may use at most 64 MiB of HBM per device.

v0:
```python
import jax
import jax.numpy as jnp
from jax import lax
from jax.sharding import PartitionSpec as P


def local(tokens, expert_ids, gate_weight, w_gate, w_up, w_down, grad_out):
    tok_dev, fanout = expert_ids.shape
    feature_cols = tokens.shape[1]
    experts = lax.axis_size("expert")
    capacity = max(2, min(tok_dev, 2 * tok_dev * fanout // (4 * experts)))
    pair_count = tok_dev * fanout
    flat_ids = expert_ids.reshape(pair_count)
    onehot = (flat_ids[:, None] == jnp.arange(experts, dtype=jnp.int32)[None, :]).astype(jnp.int32)
    before = jnp.cumsum(onehot, axis=0) - onehot
    slot_index = jnp.sum(before * onehot, axis=1)
    position = flat_ids * capacity + slot_index
    placing = jnp.arange(experts * capacity, dtype=jnp.int32)[:, None] == position[None, :]
    placing = placing.reshape(experts * capacity, tok_dev, fanout)
    select = jnp.sum(placing.astype(jnp.float32), axis=2).astype(jnp.bfloat16)
    slot_gate = jnp.sum(jnp.where(placing, gate_weight[None, :, :], 0.0), axis=(1, 2))
    x_slab = jnp.dot(select, tokens, preferred_element_type=jnp.float32).astype(jnp.bfloat16)
    x_slab = x_slab.reshape(experts, capacity, feature_cols)
    cot_rows = jnp.dot(select, grad_out, preferred_element_type=jnp.float32)
    c_slab = (slot_gate[:, None] * cot_rows).astype(jnp.bfloat16)
    c_slab = c_slab.reshape(experts, capacity, feature_cols)
    gate_mat = w_gate[0]
    up_mat = w_up[0]
    down_mat = w_down[0]
    row_total = experts * capacity
    transposed = (((1,), (1,)), ((), ()))
    arrived = lax.all_to_all(x_slab, "expert", split_axis=0, concat_axis=0, tiled=True)
    x_rows = arrived.reshape(row_total, feature_cols)
    gate_part = jnp.dot(x_rows, gate_mat, preferred_element_type=jnp.float32)
    up_part = jnp.dot(x_rows, up_mat, preferred_element_type=jnp.float32)
    gate_pre = lax.psum(gate_part.astype(jnp.bfloat16), "dp").astype(jnp.float32)
    up_pre = lax.psum(up_part.astype(jnp.bfloat16), "dp").astype(jnp.float32)
    hidden = (jax.nn.silu(gate_pre) * up_pre).astype(jnp.bfloat16)
    out_rows = jnp.dot(hidden, down_mat, preferred_element_type=jnp.float32).astype(jnp.bfloat16)
    gate_pre, up_pre, hidden, out_rows = (
        gate_pre,
        up_pre,
        hidden,
        out_rows.reshape(experts, capacity, feature_cols),
    )
    back_out = lax.all_to_all(out_rows, "expert", split_axis=0, concat_axis=0, tiled=True)
    arrived_grads = lax.all_to_all(c_slab, "expert", split_axis=0, concat_axis=0, tiled=True)
    c_rows = arrived_grads.reshape(row_total, feature_cols)
    hidden_part = lax.dot_general(c_rows, down_mat, transposed, preferred_element_type=jnp.float32)
    sig = jax.nn.sigmoid(gate_pre)
    grad_hidden = lax.psum(hidden_part.astype(jnp.bfloat16), "dp").astype(jnp.float32)
    grad_gate = (grad_hidden * up_pre * sig * (1.0 + gate_pre * (1.0 - sig))).astype(jnp.bfloat16)
    grad_up = (grad_hidden * jax.nn.silu(gate_pre)).astype(jnp.bfloat16)
    grad_rows = lax.dot_general(grad_gate, gate_mat, transposed, preferred_element_type=jnp.float32)
    grad_rows = grad_rows + lax.dot_general(
        grad_up, up_mat, transposed, preferred_element_type=jnp.float32
    )
    grad_rows = grad_rows.astype(jnp.bfloat16).reshape(experts, capacity, feature_cols)
    down_grad = lax.dot_general(
        hidden, c_rows, (((0,), (0,)), ((), ())), preferred_element_type=jnp.float32
    )
    grad_rows, down_grad = (grad_rows, down_grad.astype(jnp.bfloat16))
    back_grads = lax.all_to_all(grad_rows, "expert", split_axis=0, concat_axis=0, tiled=True)
    scaled = back_out.reshape(row_total, feature_cols).astype(jnp.float32) * slot_gate[:, None]
    upper_part = scaled.astype(jnp.bfloat16)
    lower_part = (scaled - upper_part.astype(jnp.float32)).astype(jnp.bfloat16)
    output = jnp.dot(select.T, upper_part, preferred_element_type=jnp.float32)
    output = (output + jnp.dot(select.T, lower_part, preferred_element_type=jnp.float32)).astype(
        jnp.bfloat16
    )
    grad_flat = back_grads.reshape(row_total, feature_cols)
    grad_tokens = jnp.dot(select.T, grad_flat, preferred_element_type=jnp.float32).astype(
        jnp.bfloat16
    )
    return (output, grad_tokens, down_grad.reshape(1, down_grad.shape[0], feature_cols))


def solution(mesh):
    return jax.shard_map(
        local,
        mesh=mesh,
        in_specs=(
            P("expert", "dp"),
            P("expert", None),
            P("expert", None),
            P("expert", "dp", None),
            P("expert", "dp", None),
            P("expert", None, "dp"),
            P("expert", "dp"),
        ),
        out_specs=(P("expert", "dp"), P("expert", "dp"), P("expert", None, "dp")),
        check_vma=False,
    )
```

profile of v0, /device:TPU:11, one launch (start us, length us, event | category | flops | bytes accessed | tf_op | source)
XLA Modules:
  0.0 318.3 jit_solution(14854506770356374318)
XLA Ops:
  7.2 0.8 copy.28
  8.0 0.1 eq.44
  8.1 0.1 eq.40
  8.2 4.5 %reduce-window.6 = s32[16,8,128]{2,1,0:T(8,128)S(1)} reduce-window(s32[16,8,128]{2,1,0:T(8,128)S(1)} %fusion.48, s32[]{:T(128)} %constant.12.clone.1), window={size=1x1x128 pad=0_0x0_0x127_0}, to_apply=%region_0.0 | reduce-window | flops 2080768 | bytes 131076 | tf_op jit(solution)/shard_map/reduce-window
  12.8 0.1 copy.30
  13.1 0.1 broadcast_add_fusion
  13.3 0.7 multiply_add_fusion
  14.0 2.3 select_reduce_fusion
  16.4 1.9 convolution_convert_fusion.1
  18.3 6.7 %all-to-all-start = ((bf16[16,32,1792]{2,1,0:T(8,128)(2,1)}), bf16[16,32,1792]{2,1,0:T(8,128)(2,1)S(1)}, u32[]{:S(2)}, u32[]{:S(2)}) async-start(bf16[16,32,1792]{2,1,0:T(8,128)(2,1)} %bitcast.2), calls=%async_computation | async-start | bytes 3670016 | tf_op jit(solution)/shard_map/all_to_all | solution.py:32
  24.9 1.9 multiply_convert_fusion
  26.8 39.9 %all-to-all-done = bf16[16,32,1792]{2,1,0:T(8,128)(2,1)S(1)} async-done(((bf16[16,32,1792]{2,1,0:T(8,128)(2,1)}), bf16[16,32,1792]{2,1,0:T(8,128)(2,1)S(1)}, u32[]{:S(2)}, u32[]{:S(2)}) %all-to-all-start) | async-done | bytes 1835040 | tf_op jit(solution)/shard_map/all_to_all | solution.py:32
  66.7 1.2 copy-done.4
  67.9 4.8 %all-to-all-start.2 = ((bf16[16,32,1792]{2,1,0:T(8,128)(2,1)}), bf16[16,32,1792]{2,1,0:T(8,128)(2,1)S(1)}, u32[]{:S(2)}, u32[]{:S(2)}) async-start(bf16[16,32,1792]{2,1,0:T(8,128)(2,1)} %bitcast.9), calls=%async_computation.2 | async-start | bytes 3670016 | tf_op jit(solution)/shard_map/all_to_all | solution.py:47
  72.8 5.8 %fusion.36 = bf16[512,1024]{1,0:T(8,128)(2,1)} fusion(bf16[512,1792]{1,0:T(8,128)(2,1)} %bitcast.71, bf16[1,1792,1024]{2,1,0:T(8,128)(2,1)} %param.11), kind=kOutput, calls=%fused_computation.45 | convolution fusion | flops 1879572480 | bytes 6553600 | tf_op jit(solution)/shard_map/dot_general | solution.py:35
  78.6 3.0 fusion.33
  81.6 32.9 %all-to-all-done.2 = bf16[16,32,1792]{2,1,0:T(8,128)(2,1)S(1)} async-done(((bf16[16,32,1792]{2,1,0:T(8,128)(2,1)}), bf16[16,32,1792]{2,1,0:T(8,128)(2,1)S(1)}, u32[]{:S(2)}, u32[]{:S(2)}) %all-to-all-start.2) | async-done | bytes 1835040 | tf_op jit(solution)/shard_map/all_to_all | solution.py:47
  114.5 5.8 %fusion.39 = bf16[512,1024]{1,0:T(8,128)(2,1)} fusion(bf16[512,1792]{1,0:T(8,128)(2,1)S(1)} %bitcast.69, bf16[1,1024,1792]{2,1,0:T(8,128)(2,1)} %param.12), kind=kOutput, calls=%fused_computation.46 | convolution fusion | flops 1879572480 | bytes 6553600 | tf_op jit(solution)/shard_map/dot_general | solution.py:49
  120.3 85.3 %all-reduce.3.cloned.1.call-done = (bf16[512,1024]{1,0:T(8,128)(2,1)}, bf16[512,1024]{1,0:T(8,128)(2,1)}, bf16[512,1024]{1,0:T(8,128)(2,1)}) async-done(((bf16[512,1024]{1,0:T(8,128)(2,1)}, bf16[512,1024]{1,0:T(8,128)(2,1)}, bf16[512,1024]{1,0:T(8,128)(2,1)}), (bf16[512,1024]{1,0:T(8,128)(2,1)}, bf16[512,1024]{1,0:T(8,128)(2,1)}, bf16[512,1024]{1,0:T(8,128)(2,1)})) %all-reduce.3.cloned.1.call-update) | async-done | bytes 3145744 | tf_op jit(solution)/shard_map/psum | solution.py:37
  205.6 6.4 %fusion.18 = bf16[512,1792]{1,0:T(8,128)(2,1)} fusion(bf16[1,1024,1792]{2,1,0:T(8,128)(2,1)} %param.12, bf16[512,1024]{1,0:T(8,128)(2,1)} %get-tuple-element.5, bf16[512,1024]{1,0:T(8,128)(2,1)} %get-tuple-element.6), kind=kOutput, calls=%fused_computation.23 | convolution fusion | flops 1884160000 | bytes 7602176 | tf_op jit(solution)/shard_map/dot_general | solution.py:39
  212.0 6.5 %all-to-all-start.1 = ((bf16[16,32,1792]{2,1,0:T(8,128)(2,1)}), bf16[16,32,1792]{2,1,0:T(8,128)(2,1)S(1)}, u32[]{:S(2)}, u32[]{:S(2)}) async-start(bf16[16,32,1792]{2,1,0:T(8,128)(2,1)} %bitcast.74), calls=%async_computation.1 | async-start | bytes 3670016 | tf_op jit(solution)/shard_map/all_to_all | solution.py:46
  218.5 5.3 %fusion.7 = f32[512,1792]{1,0:T(8,128)S(1)} fusion(bf16[1,1792,1024]{2,1,0:T(8,128)(2,1)} %param.11, bf16[512,1024]{1,0:T(8,128)(2,1)} %get-tuple-element.7, bf16[512,1024]{1,0:T(8,128)(2,1)} %get-tuple-element.6), kind=kOutput, calls=%fused_computation.9 | convolution fusion | flops 1883242496 | bytes 9437184 | tf_op jit(solution)/shard_map/dot_general | solution.py:55
  223.8 4.2 %add_convert_fusion = bf16[512,1792]{1,0:T(8,128)(2,1)} fusion(f32[512,1792]{1,0:T(8,128)S(1)} %fusion.7, bf16[1,1792,1024]{2,1,0:T(8,128)(2,1)S(1)} %copy-done.8, bf16[512,1024]{1,0:T(8,128)(2,1)S(1)} %copy-done.9, bf16[512,1024]{1,0:T(8,128)(2,1)S(1)} %copy-done.11, bf16[512,1024]{1,0:T(8,128)(2,1)S(1)} %copy-done.10), kind=kOutput, calls=%fused_computation.17 | convolution fusion | flops 1887698944 | bytes 12320768 | tf_op jit(solution)/shard_map/dot_general | solution.py:54
  228.0 32.3 %all-to-all-done.1 = bf16[16,32,1792]{2,1,0:T(8,128)(2,1)S(1)} async-done(((bf16[16,32,1792]{2,1,0:T(8,128)(2,1)}), bf16[16,32,1792]{2,1,0:T(8,128)(2,1)S(1)}, u32[]{:S(2)}, u32[]{:S(2)}) %all-to-all-start.1) | async-done | bytes 1835040 | tf_op jit(solution)/shard_map/all_to_all | solution.py:46
  260.3 4.8 %all-to-all-start.3 = ((bf16[16,32,1792]{2,1,0:T(8,128)(2,1)}), bf16[16,32,1792]{2,1,0:T(8,128)(2,1)}, u32[]{:S(2)}, u32[]{:S(2)}) async-start(bf16[16,32,1792]{2,1,0:T(8,128)(2,1)} %bitcast.73), calls=%async_computation.3 | async-start | bytes 3670016 | tf_op jit(solution)/shard_map/all_to_all | solution.py:63
  265.0 6.2 %fusion.15 = bf16[1,1024,1792]{2,1,0:T(8,128)(2,1)} fusion(bf16[512,1792]{1,0:T(8,128)(2,1)} %bitcast.70, bf16[512,1024]{1,0:T(8,128)(2,1)} %get-tuple-element.5, bf16[512,1024]{1,0:T(8,128)(2,1)} %get-tuple-element.6), kind=kOutput, calls=%fused_computation.19 | convolution fusion | flops 1885077504 | bytes 7602176 | tf_op jit(solution)/shard_map/dot_general | solution.py:59
  271.3 0.4 fusion.1
  271.7 1.2 copy-done.1
  272.9 0.4 fusion.53
  273.3 33.6 %all-to-all-done.3 = bf16[16,32,1792]{2,1,0:T(8,128)(2,1)} async-done(((bf16[16,32,1792]{2,1,0:T(8,128)(2,1)}), bf16[16,32,1792]{2,1,0:T(8,128)(2,1)}, u32[]{:S(2)}, u32[]{:S(2)}) %all-to-all-start.3) | async-done | bytes 1835040 | tf_op jit(solution)/shard_map/all_to_all | solution.py:63
  306.9 2.8 convolution_convert_fusion.2
  309.8 1.7 fusion.21
  (32 shorter events, 0.4 us)
Async XLA Ops:
  7.2 9.2 %copy-start = (bf16[128,1792]{1,0:T(8,128)(2,1)S(1)}, bf16[128,1792]{1,0:T(8,128)(2,1)}, u32[]{:S(2)}) copy-start(bf16[128,1792]{1,0:T(8,128)(2,1)} %param.7) | copy-start | bytes 1376260
  18.2 6.7 %copy-start.6 = (bf16[128,1792]{1,0:T(8,128)(2,1)S(1)}, bf16[128,1792]{1,0:T(8,128)(2,1)}, u32[]{:S(2)}) copy-start(bf16[128,1792]{1,0:T(8,128)(2,1)} %param.13) | copy-start | bytes 1376260
  18.3 48.5 %all-to-all-start = ((bf16[16,32,1792]{2,1,0:T(8,128)(2,1)}), bf16[16,32,1792]{2,1,0:T(8,128)(2,1)S(1)}, u32[]{:S(2)}, u32[]{:S(2)}) async-start(bf16[16,32,1792]{2,1,0:T(8,128)(2,1)} %bitcast.2), calls=%async_computation | async-start | bytes 3670016 | tf_op jit(solution)/shard_map/all_to_all | solution.py:32
  66.7 1.2 copy-start.4
  67.9 46.6 %all-to-all-start.2 = ((bf16[16,32,1792]{2,1,0:T(8,128)(2,1)}), bf16[16,32,1792]{2,1,0:T(8,128)(2,1)S(1)}, u32[]{:S(2)}, u32[]{:S(2)}) async-start(bf16[16,32,1792]{2,1,0:T(8,128)(2,1)} %bitcast.9), calls=%async_computation.2 | async-start | bytes 3670016 | tf_op jit(solution)/shard_map/all_to_all | solution.py:47
  72.7 132.9 %all-reduce.3.cloned.1.call-start = ((), (), s32[]{:S(2)}) async-start(), calls=%async_computation.4 | async-start | bytes 6291456 | tf_op jit(solution)/shard_map/psum | solution.py:37
  72.8 5.8 %copy-start.5 = (bf16[16,32,1792]{2,1,0:T(8,128)(2,1)S(1)}, bf16[16,32,1792]{2,1,0:T(8,128)(2,1)}, u32[]{:S(2)}) copy-start(bf16[16,32,1792]{2,1,0:T(8,128)(2,1)} %copy-done.4) | copy-start | bytes 5505028
  72.8 5.8 %copy-start.7 = (bf16[1,1792,1024]{2,1,0:T(8,128)(2,1)S(1)}, bf16[1,1792,1024]{2,1,0:T(8,128)(2,1)}, u32[]{:S(2)}) copy-start(bf16[1,1792,1024]{2,1,0:T(8,128)(2,1)} %param.10) | copy-start | bytes 11010052
  114.5 5.8 %copy-start.3 = (bf16[16,32,1792]{2,1,0:T(8,128)(2,1)}, bf16[16,32,1792]{2,1,0:T(8,128)(2,1)S(1)}, u32[]{:S(2)}) copy-start(bf16[16,32,1792]{2,1,0:T(8,128)(2,1)S(1)} %all-to-all-done.2) | copy-start | bytes 5505028
  212.0 48.3 %all-to-all-start.1 = ((bf16[16,32,1792]{2,1,0:T(8,128)(2,1)}), bf16[16,32,1792]{2,1,0:T(8,128)(2,1)S(1)}, u32[]{:S(2)}, u32[]{:S(2)}) async-start(bf16[16,32,1792]{2,1,0:T(8,128)(2,1)} %bitcast.74), calls=%async_computation.1 | async-start | bytes 3670016 | tf_op jit(solution)/shard_map/all_to_all | solution.py:46
  218.5 5.3 %copy-start.8 = (bf16[1,1792,1024]{2,1,0:T(8,128)(2,1)S(1)}, bf16[1,1792,1024]{2,1,0:T(8,128)(2,1)}, u32[]{:S(2)}) copy-start(bf16[1,1792,1024]{2,1,0:T(8,128)(2,1)} %param.10) | copy-start | bytes 11010052
  218.5 5.3 %copy-start.9 = (bf16[512,1024]{1,0:T(8,128)(2,1)S(1)}, bf16[512,1024]{1,0:T(8,128)(2,1)}, u32[]{:S(2)}) copy-start(bf16[512,1024]{1,0:T(8,128)(2,1)} %get-tuple-element.5) | copy-start | bytes 3145732
  218.5 5.3 %copy-start.10 = (bf16[512,1024]{1,0:T(8,128)(2,1)S(1)}, bf16[512,1024]{1,0:T(8,128)(2,1)}, u32[]{:S(2)}) copy-start(bf16[512,1024]{1,0:T(8,128)(2,1)} %get-tuple-element.6) | copy-start | bytes 3145732
  218.5 5.3 %copy-start.11 = (bf16[512,1024]{1,0:T(8,128)(2,1)S(1)}, bf16[512,1024]{1,0:T(8,128)(2,1)}, u32[]{:S(2)}) copy-start(bf16[512,1024]{1,0:T(8,128)(2,1)} %get-tuple-element.7) | copy-start | bytes 3145732
  260.3 46.7 %all-to-all-start.3 = ((bf16[16,32,1792]{2,1,0:T(8,128)(2,1)}), bf16[16,32,1792]{2,1,0:T(8,128)(2,1)}, u32[]{:S(2)}, u32[]{:S(2)}) async-start(bf16[16,32,1792]{2,1,0:T(8,128)(2,1)} %bitcast.73), calls=%async_computation.3 | async-start | bytes 3670016 | tf_op jit(solution)/shard_map/all_to_all | solution.py:63
  271.7 1.2 copy-start.1
  306.9 2.8 copy-start.2
Sparse Core Ops, SparseCore 0:
  120.4 85.1 all-reduce.2
where the time goes:
time: 319 us; the launch traced here: 318 us
  waiting for transfers between devices  224 us (70%)
  matrix products  45.3 us (14%)
  starting transfers between devices  22.8 us (7%)
  between operations  14.2 us (4%)
  other arithmetic  8.11 us (3%)
  local copies, waits for them, and re-layouts  3.94 us (1%)
    psum x1, waiting for transfers between devices, local(): up_pre = lax.psum(up_part.astype(jnp.bfloat16), 'dp').astype(jnp.float32)  85.3 us
    all_to_all x1, waiting for transfers between devices, local(): lax.all_to_all(x_slab, 'expert', split_axis=0, concat_axis=0, tiled=True)  39.9 us
    all_to_all x1, waiting for transfers between devices, local(): lax.all_to_all(grad_rows, 'expert', split_axis=0, concat_axis=0, tiled=True)  33.6 us
    all_to_all x1, waiting for transfers between devices, local(): lax.all_to_all(c_slab, 'expert', split_axis=0, concat_axis=0, tiled=True)  32.9 us
    all_to_all x1, waiting for transfers between devices, local(): lax.all_to_all(out_rows, 'expert', split_axis=0, concat_axis=0, tiled=True)  32.3 us
    all_to_all x1, starting transfers between devices, local(): lax.all_to_all(x_slab, 'expert', split_axis=0, concat_axis=0, tiled=True)  6.65 us
    all_to_all x1, starting transfers between devices, local(): lax.all_to_all(out_rows, 'expert', split_axis=0, concat_axis=0, tiled=True)  6.51 us
  transfers between devices with their start and end apart: 5, of which 5 were waited for; matrix products, arithmetic and copies ran while one was open for 9% of the time, Pallas kernels for 0%

commit v1 on v0

--- a/solution.py
+++ b/solution.py
@@ -2,6 +2,11 @@
 import jax.numpy as jnp
 from jax import lax
 from jax.sharding import PartitionSpec as P
+
+
+def add_all(value, mesh_axis):
+    parts = lax.all_gather(value, mesh_axis)
+    return jnp.sum(parts, axis=0)
 
 
 def local(tokens, expert_ids, gate_weight, w_gate, w_up, w_down, grad_out):
@@ -34,7 +39,7 @@
     gate_part = jnp.dot(x_rows, gate_mat, preferred_element_type=jnp.float32)
     up_part = jnp.dot(x_rows, up_mat, preferred_element_type=jnp.float32)
     gate_pre = lax.psum(gate_part.astype(jnp.bfloat16), "dp").astype(jnp.float32)
-    up_pre = lax.psum(up_part.astype(jnp.bfloat16), "dp").astype(jnp.float32)
+    up_pre = add_all(up_part.astype(jnp.bfloat16), "dp").astype(jnp.float32)
     hidden = (jax.nn.silu(gate_pre) * up_pre).astype(jnp.bfloat16)
     out_rows = jnp.dot(hidden, down_mat, preferred_element_type=jnp.float32).astype(jnp.bfloat16)
     gate_pre, up_pre, hidden, out_rows = (

time: 319 us -> 332 us (1.041)
  waiting for transfers between devices: 224 us -> 231 us
  matrix products: 45.3 us -> 50.2 us
    psum x1, waiting for transfers between devices: 85.3 us -> 56.4 us  [local(): lax.psum(gate_part.astype(jnp.bfloat16), 'dp').astype(jnp.float32)]
    all_gather x0 -> x1, waiting for transfers between devices: none -> 27.7 us  [add_all(): parts = lax.all_gather(value, mesh_axis)]
    all_to_all x1, waiting for transfers between devices: 32.9 us -> 39.9 us  [local(): lax.all_to_all(c_slab, 'expert', split_axis=0, concat_axis=0, tiled=True)]
    dot_general x1, matrix products: 4.16 us -> 7.57 us  [local(): lax.dot_general(grad_gate, gate_mat, transposed, preferred_element_type=j...]
  transfers between devices with their start and end apart: 5 -> 6, of which waited for: 5 -> 6; matrix products, arithmetic and copies ran while one was open for 9% -> 10% of each run, Pallas kernels for 0% -> 0%
where the time goes in v1:
time: 332 us; the launch traced here: 331 us
  waiting for transfers between devices  231 us (70%)
  matrix products  50.2 us (15%)
  starting transfers between devices  23 us (7%)
  between operations  14.1 us (4%)
  other arithmetic  10.3 us (3%)
    psum x1, waiting for transfers between devices, local(): lax.psum(gate_part.astype(jnp.bfloat16), 'dp').astype(jnp.float32)  56.4 us
    all_to_all x1, waiting for transfers between devices, local(): lax.all_to_all(c_slab, 'expert', split_axis=0, concat_axis=0, tiled=True)  39.9 us
    all_to_all x1, waiting for transfers between devices, local(): lax.all_to_all(x_slab, 'expert', split_axis=0, concat_axis=0, tiled=True)  36.7 us
    all_to_all x1, waiting for transfers between devices, local(): lax.all_to_all(grad_rows, 'expert', split_axis=0, concat_axis=0, tiled=True)  35.7 us
    all_to_all x1, waiting for transfers between devices, local(): lax.all_to_all(out_rows, 'expert', split_axis=0, concat_axis=0, tiled=True)  34.6 us
    all_gather x1, waiting for transfers between devices, add_all(): parts = lax.all_gather(value, mesh_axis)  27.7 us
    dot_general x1, matrix products, local(): lax.dot_general(grad_gate, gate_mat, transposed, preferred_element_type=j...  7.57 us
    dot_general x1, matrix products, local(): lax.dot_general(grad_up, up_mat, transposed, preferred_element_type=jnp.f...  7 us
  transfers between devices with their start and end apart: 6, of which 6 were waited for; matrix products, arithmetic and copies ran while one was open for 10% of the time, Pallas kernels for 0%

profile of v1, /device:TPU:11, one launch (start us, length us, event | category | flops | bytes accessed | tf_op | source)
XLA Modules:
  0.0 331.4 jit_solution(2727360676831782622)
XLA Ops:
  7.2 0.8 copy.28
  8.0 0.1 eq.44
  8.2 4.5 %reduce-window.6 = s32[16,8,128]{2,1,0:T(8,128)S(1)} reduce-window(s32[16,8,128]{2,1,0:T(8,128)S(1)} %fusion.48, s32[]{:T(128)} %constant.13.clone.1), window={size=1x1x128 pad=0_0x0_0x127_0}, to_apply=%region_0.0 | reduce-window | flops 2080768 | bytes 131076 | tf_op jit(solution)/shard_map/reduce-window
  12.8 0.1 copy.30
  13.3 0.7 multiply_add_fusion
  14.0 2.3 select_reduce_fusion
  16.4 1.9 multiply_convert_fusion
  18.3 6.7 %all-to-all-start.2 = ((bf16[16,32,1792]{2,1,0:T(8,128)(2,1)}), bf16[16,32,1792]{2,1,0:T(8,128)(2,1)S(1)}, u32[]{:S(2)}, u32[]{:S(2)}) async-start(bf16[16,32,1792]{2,1,0:T(8,128)(2,1)} %bitcast.10), calls=%async_computation.2 | async-start | bytes 3670016 | tf_op jit(solution)/shard_map/all_to_all | solution.py:52
  25.0 1.8 convolution_convert_fusion.1
  26.8 39.9 %all-to-all-done.2 = bf16[16,32,1792]{2,1,0:T(8,128)(2,1)S(1)} async-done(((bf16[16,32,1792]{2,1,0:T(8,128)(2,1)}), bf16[16,32,1792]{2,1,0:T(8,128)(2,1)S(1)}, u32[]{:S(2)}, u32[]{:S(2)}) %all-to-all-start.2) | async-done | bytes 1835040 | tf_op jit(solution)/shard_map/all_to_all | solution.py:52
  66.8 4.8 %all-to-all-start = ((bf16[16,32,1792]{2,1,0:T(8,128)(2,1)}), bf16[16,32,1792]{2,1,0:T(8,128)(2,1)}, u32[]{:S(2)}, u32[]{:S(2)}) async-start(bf16[16,32,1792]{2,1,0:T(8,128)(2,1)} %bitcast.2), calls=%async_computation | async-start | bytes 3670016 | tf_op jit(solution)/shard_map/all_to_all | solution.py:37
  71.6 5.1 %fusion.39 = bf16[512,1024]{1,0:T(8,128)(2,1)} fusion(bf16[512,1792]{1,0:T(8,128)(2,1)S(1)} %bitcast.72, bf16[1,1024,1792]{2,1,0:T(8,128)(2,1)} %param.12), kind=kOutput, calls=%fused_computation.46 | convolution fusion | flops 1879572480 | bytes 6553600 | tf_op jit(solution)/shard_map/dot_general | solution.py:54
  76.7 36.7 %all-to-all-done = bf16[16,32,1792]{2,1,0:T(8,128)(2,1)} async-done(((bf16[16,32,1792]{2,1,0:T(8,128)(2,1)}), bf16[16,32,1792]{2,1,0:T(8,128)(2,1)}, u32[]{:S(2)}, u32[]{:S(2)}) %all-to-all-start) | async-done | bytes 1835040 | tf_op jit(solution)/shard_map/all_to_all | solution.py:37
  113.4 5.6 %fusion.33 = bf16[512,1024]{1,0:T(8,128)(2,1)} fusion(bf16[512,1792]{1,0:T(8,128)(2,1)} %bitcast.3, bf16[1,1792,1024]{2,1,0:T(8,128)(2,1)} %param.10), kind=kOutput, calls=%fused_computation.44 | convolution fusion | flops 1879572480 | bytes 6553600 | tf_op jit(solution)/shard_map/dot_general | solution.py:39
  119.1 0.2 all-gather.3.cloned.1.call-start
  119.3 5.7 %fusion.36 = bf16[512,1024]{1,0:T(8,128)(2,1)} fusion(bf16[512,1792]{1,0:T(8,128)(2,1)} %bitcast.3, bf16[1,1792,1024]{2,1,0:T(8,128)(2,1)} %param.11), kind=kOutput, calls=%fused_computation.45 | convolution fusion | flops 1879572480 | bytes 6553600 | tf_op jit(solution)/shard_map/dot_general | solution.py:40
  125.1 56.4 %all-reduce.3.cloned.1.call-done = (bf16[512,1024]{1,0:T(8,128)(2,1)}, bf16[512,1024]{1,0:T(8,128)(2,1)}) async-done(((bf16[512,1024]{1,0:T(8,128)(2,1)}, bf16[512,1024]{1,0:T(8,128)(2,1)}), (bf16[512,1024]{1,0:T(8,128)(2,1)}, bf16[512,1024]{1,0:T(8,128)(2,1)})) %all-reduce.3.cloned.1.call-update) | async-done | bytes 2097168 | tf_op jit(solution)/shard_map/psum | solution.py:41
  181.5 7.0 %fusion.7 = f32[512,1792]{1,0:T(8,128)} fusion(bf16[1,1792,1024]{2,1,0:T(8,128)(2,1)} %param.11, bf16[512,1024]{1,0:T(8,128)(2,1)} %get-tuple-element.6, bf16[512,1024]{1,0:T(8,128)(2,1)} %get-tuple-element.5), kind=kOutput, calls=%fused_computation.9 | convolution fusion | flops 1883242496 | bytes 9437184 | tf_op jit(solution)/shard_map/dot_general | solution.py:60
  188.5 27.7 %all-gather.3.cloned.1.call-done = bf16[1024,1024]{1,0:T(8,128)(2,1)} async-done(((bf16[512,1024]{1,0:T(8,128)(2,1)}), bf16[1024,1024]{1,0:T(8,128)(2,1)}) %all-gather.3.cloned.1.call-update) | async-done | bytes 2097168 | tf_op jit(solution)/shard_map/all_gather | solution.py:8
  216.2 2.2 reduce_sum.44
  218.3 7.6 %add_convert_fusion = bf16[512,1792]{1,0:T(8,128)(2,1)} fusion(f32[512,1792]{1,0:T(8,128)} %fusion.7, bf16[1,1792,1024]{2,1,0:T(8,128)(2,1)} %param.10, bf16[512,1024]{1,0:T(8,128)(2,1)S(1)} %reduce_sum.44, bf16[512,1024]{1,0:T(8,128)(2,1)} %get-tuple-element.6, bf16[512,1024]{1,0:T(8,128)(2,1)S(1)} %copy-done.5), kind=kOutput, calls=%fused_computation.17 | convolution fusion | flops 1887698944 | bytes 12320768 | tf_op jit(solution)/shard_map/dot_general | solution.py:59
  225.9 6.5 %all-to-all-start.3 = ((bf16[16,32,1792]{2,1,0:T(8,128)(2,1)}), bf16[16,32,1792]{2,1,0:T(8,128)(2,1)S(1)}, u32[]{:S(2)}, u32[]{:S(2)}) async-start(bf16[16,32,1792]{2,1,0:T(8,128)(2,1)} %bitcast.75), calls=%async_computation.3 | async-start | bytes 3670016 | tf_op jit(solution)/shard_map/all_to_all | solution.py:68
  232.4 6.1 %fusion.18 = bf16[512,1792]{1,0:T(8,128)(2,1)} fusion(bf16[1,1024,1792]{2,1,0:T(8,128)(2,1)} %param.12, bf16[512,1024]{1,0:T(8,128)(2,1)S(1)} %reduce_sum.44, bf16[512,1024]{1,0:T(8,128)(2,1)} %get-tuple-element.5), kind=kOutput, calls=%fused_computation.23 | convolution fusion | flops 1884160000 | bytes 7602176 | tf_op jit(solution)/shard_map/dot_general | solution.py:44
  238.5 35.7 %all-to-all-done.3 = bf16[16,32,1792]{2,1,0:T(8,128)(2,1)S(1)} async-done(((bf16[16,32,1792]{2,1,0:T(8,128)(2,1)}), bf16[16,32,1792]{2,1,0:T(8,128)(2,1)S(1)}, u32[]{:S(2)}, u32[]{:S(2)}) %all-to-all-start.3) | async-done | bytes 1835040 | tf_op jit(solution)/shard_map/all_to_all | solution.py:68
  274.2 1.3 copy-done.1
  275.5 4.8 %all-to-all-start.1 = ((bf16[16,32,1792]{2,1,0:T(8,128)(2,1)}), bf16[16,32,1792]{2,1,0:T(8,128)(2,1)S(1)}, u32[]{:S(2)}, u32[]{:S(2)}) async-start(bf16[16,32,1792]{2,1,0:T(8,128)(2,1)} %bitcast.74), calls=%async_computation.1 | async-start | bytes 3670016 | tf_op jit(solution)/shard_map/all_to_all | solution.py:51
  280.3 6.0 %fusion.15 = bf16[1,1024,1792]{2,1,0:T(8,128)(2,1)} fusion(bf16[512,1792]{1,0:T(8,128)(2,1)} %bitcast.73, bf16[512,1024]{1,0:T(8,128)(2,1)S(1)} %reduce_sum.44, bf16[512,1024]{1,0:T(8,128)(2,1)} %get-tuple-element.5), kind=kOutput, calls=%fused_computation.19 | convolution fusion | flops 1885077504 | bytes 7602176 | tf_op jit(solution)/shard_map/dot_general | solution.py:64
  286.3 1.2 convolution_convert_fusion.2
  287.5 34.6 %all-to-all-done.1 = bf16[16,32,1792]{2,1,0:T(8,128)(2,1)S(1)} async-done(((bf16[16,32,1792]{2,1,0:T(8,128)(2,1)}), bf16[16,32,1792]{2,1,0:T(8,128)(2,1)S(1)}, u32[]{:S(2)}, u32[]{:S(2)}) %all-to-all-start.1) | async-done | bytes 1835040 | tf_op jit(solution)/shard_map/all_to_all | solution.py:51
  322.1 0.4 fusion.1
  322.5 0.4 fusion.53
  322.9 1.7 fusion.21
  (24 shorter events, 0.6 us)
Async XLA Ops:
  7.2 9.2 %copy-start = (bf16[128,1792]{1,0:T(8,128)(2,1)S(1)}, bf16[128,1792]{1,0:T(8,128)(2,1)}, u32[]{:S(2)}) copy-start(bf16[128,1792]{1,0:T(8,128)(2,1)} %param.13) | copy-start | bytes 1376260
  18.3 6.7 %copy-start.4 = (bf16[128,1792]{1,0:T(8,128)(2,1)S(1)}, bf16[128,1792]{1,0:T(8,128)(2,1)}, u32[]{:S(2)}) copy-start(bf16[128,1792]{1,0:T(8,128)(2,1)} %param.7) | copy-start | bytes 1376260
  18.3 48.5 %all-to-all-start.2 = ((bf16[16,32,1792]{2,1,0:T(8,128)(2,1)}), bf16[16,32,1792]{2,1,0:T(8,128)(2,1)S(1)}, u32[]{:S(2)}, u32[]{:S(2)}) async-start(bf16[16,32,1792]{2,1,0:T(8,128)(2,1)} %bitcast.10), calls=%async_computation.2 | async-start | bytes 3670016 | tf_op jit(solution)/shard_map/all_to_all | solution.py:52
  66.8 9.9 %copy-start.3 = (bf16[16,32,1792]{2,1,0:T(8,128)(2,1)}, bf16[16,32,1792]{2,1,0:T(8,128)(2,1)S(1)}, u32[]{:S(2)}) copy-start(bf16[16,32,1792]{2,1,0:T(8,128)(2,1)S(1)} %all-to-all-done.2) | copy-start | bytes 5505028
  66.8 46.7 %all-to-all-start = ((bf16[16,32,1792]{2,1,0:T(8,128)(2,1)}), bf16[16,32,1792]{2,1,0:T(8,128)(2,1)}, u32[]{:S(2)}, u32[]{:S(2)}) async-start(bf16[16,32,1792]{2,1,0:T(8,128)(2,1)} %bitcast.2), calls=%async_computation | async-start | bytes 3670016 | tf_op jit(solution)/shard_map/all_to_all | solution.py:37
  71.5 110.0 %all-reduce.3.cloned.1.call-start = ((), (), s32[]{:S(2)}) async-start(), calls=%async_computation.5 | async-start | bytes 4194304 | tf_op jit(solution)/shard_map/psum | solution.py:41
  119.1 97.1 %all-gather.3.cloned.1.call-start = ((), (), s32[]{:S(2)}) async-start(), calls=%async_computation.4 | async-start | bytes 3145728 | tf_op jit(solution)/shard_map/all_gather | solution.py:8
  188.5 29.8 %copy-start.5 = (bf16[512,1024]{1,0:T(8,128)(2,1)S(1)}, bf16[512,1024]{1,0:T(8,128)(2,1)}, u32[]{:S(2)}) copy-start(bf16[512,1024]{1,0:T(8,128)(2,1)} %get-tuple-element.5) | copy-start | bytes 3145732
  225.9 48.3 %all-to-all-start.3 = ((bf16[16,32,1792]{2,1,0:T(8,128)(2,1)}), bf16[16,32,1792]{2,1,0:T(8,128)(2,1)S(1)}, u32[]{:S(2)}, u32[]{:S(2)}) async-start(bf16[16,32,1792]{2,1,0:T(8,128)(2,1)} %bitcast.75), calls=%async_computation.3 | async-start | bytes 3670016 | tf_op jit(solution)/shard_map/all_to_all | solution.py:68
  274.2 1.3 copy-start.1
  275.5 46.6 %all-to-all-start.1 = ((bf16[16,32,1792]{2,1,0:T(8,128)(2,1)}), bf16[16,32,1792]{2,1,0:T(8,128)(2,1)S(1)}, u32[]{:S(2)}, u32[]{:S(2)}) async-start(bf16[16,32,1792]{2,1,0:T(8,128)(2,1)} %bitcast.74), calls=%async_computation.1 | async-start | bytes 3670016 | tf_op jit(solution)/shard_map/all_to_all | solution.py:51
  280.3 6.0 %copy-start.2 = (bf16[16,32,1792]{2,1,0:T(8,128)(2,1)S(1)}, bf16[16,32,1792]{2,1,0:T(8,128)(2,1)}, u32[]{:S(2)}) copy-start(bf16[16,32,1792]{2,1,0:T(8,128)(2,1)} %copy-done.1) | copy-start | bytes 5505028
Sparse Core Ops, SparseCore 0:
  119.2 62.2 all-reduce.2
  183.0 33.0 all-gather.2
